TPU v7x, 512 devices: a whole 4x4x16 slice. The times are simulated.
512 devices in a mesh: ctx: 16 (over z_lo, core), tp: 4 (over x), dp: 8 (over y, z_hi).
Axes of the slice: x: 4, y: 4, z: 16 (z_hi: 2, z_lo: 8; z = z_hi * 8 + z_lo), core: 2. Of those that a mesh axis runs over, the one named last changes fastest.
Arguments:
- queries: bfloat16 [8192, 8192], P(('dp', 'ctx'), 'tp'), parts along dimension 0, may hold values from -12 to 12
- cache_keys: bfloat16 [65536, 1024], P(('dp', 'ctx'), 'tp'), parts along dimension 0, may hold values from -4 to 4
- cache_values: bfloat16 [65536, 1024], P(('dp', 'ctx'), 'tp'), parts along dimension 0, may hold values from -6 to 6
- new_keys: bfloat16 [8192, 1024], P(('dp', 'ctx'), 'tp'), parts along dimension 0, may hold values from -6 to 6
- new_values: bfloat16 [8192, 1024], P(('dp', 'ctx'), 'tp'), parts along dimension 0, may hold values from -6 to 6
- prefix_len: int32 [8], P('dp'), parts along dimension 0, may hold values from 4096 to 8192
Outputs:
- attended: bfloat16 [8192, 8192], P(('dp', 'ctx'), 'tp'), parts along dimension 0
There are 8 independent parts, one for each index of `dp`. A program takes and returns all parts, laid end to end along the dimension named above; each array names one. Nothing has to cross between parts.
All inputs are finite; a program needn't handle non-finite values.
Results may differ from a plain program's by a relative error of at most 0.038.
Values may be sent and summed in bfloat16 or wider, within the bound.
A program may use at most 64 MiB of HBM per device.

v0:
```python
import jax
import jax.numpy as jnp
from jax import lax
from jax.sharding import PartitionSpec as P

HEAD_DIM = 128


def passed_along(value, axis, steps):
    count = lax.axis_size(axis)
    pairs = [(source, (source + steps) % count) for source in range(count)]
    return lax.ppermute(value, axis, pairs)


def allowed_for(source, query_tok, cache_rows, query_rows, length):
    key_rows = cache_rows + query_rows
    key_index = jnp.arange(key_rows, dtype=jnp.int32)
    cache_pos = source * cache_rows + key_index
    new_pos = source * query_rows + key_index - cache_rows
    return jnp.where(
        (key_index < cache_rows)[None, :],
        (cache_pos < length)[None, :],
        new_pos[None, :] <= query_tok[:, None],
    )


def softmax_block(running, query_heads, kv_block, allowed):
    old_max, old_total, old_acc = running
    scale = HEAD_DIM ** (-0.5)
    scores = (
        jnp.einsum("hrd,hkd->hrk", query_heads, kv_block[0], preferred_element_type=jnp.float32)
        * scale
    )
    scores = jnp.where(allowed[None], scores, jnp.float32(-1e30))
    new_max = jnp.maximum(old_max, jnp.max(scores, -1))
    weights = jnp.where(allowed[None], jnp.exp(scores - new_max[..., None]), jnp.float32(0.0))
    rescale = jnp.exp(old_max - new_max)
    new_total = old_total * rescale + jnp.sum(weights, -1)
    new_acc = old_acc * rescale[..., None] + jnp.einsum(
        "hrk,hkd->hrd",
        weights.astype(jnp.bfloat16),
        kv_block[1],
        preferred_element_type=jnp.float32,
    )
    return (new_max, new_total, new_acc)


def empty_state(heads, rows):
    return (
        jnp.full((heads, rows), -1e30, jnp.float32),
        jnp.zeros((heads, rows), jnp.float32),
        jnp.zeros((heads, rows, HEAD_DIM), jnp.float32),
    )


def local(queries, cache_keys, cache_values, new_keys, new_values, prefix_len):
    length = prefix_len[0]
    cycle_size = lax.axis_size("ctx")
    my_index = lax.axis_index("ctx")
    cache_rows = cache_keys.shape[0]
    query_rows = queries.shape[0]
    kv_width = cache_keys.shape[1]
    kv_heads = kv_width // HEAD_DIM
    groups = queries.shape[1] // kv_width
    key_rows = cache_rows + query_rows
    stacked = jnp.stack(
        [jnp.concatenate([cache_keys, new_keys], 0), jnp.concatenate([cache_values, new_values], 0)]
    )
    kv_block = stacked.reshape(2, key_rows, kv_heads, HEAD_DIM).transpose(0, 2, 1, 3)
    query_heads = (
        queries.reshape(query_rows, kv_heads, groups, HEAD_DIM)
        .transpose(1, 0, 2, 3)
        .reshape(kv_heads, query_rows * groups, HEAD_DIM)
    )
    query_tok = my_index * query_rows + jnp.arange(query_rows * groups, dtype=jnp.int32) // groups
    running = softmax_block(
        empty_state(kv_heads, query_rows * groups),
        query_heads,
        kv_block,
        allowed_for(my_index, query_tok, cache_rows, query_rows, length),
    )

    def one_turn(turn_index, loop_state):
        running_now, held = loop_state
        held = passed_along(held, "ctx", 1)
        source = (my_index - turn_index) % cycle_size
        allowed = allowed_for(source, query_tok, cache_rows, query_rows, length)
        return (softmax_block(running_now, query_heads, held, allowed), held)

    running, held = lax.fori_loop(1, cycle_size, one_turn, (running, kv_block))
    final_max, final_total, final_acc = running
    result = final_acc / final_total[..., None]
    result = result.reshape(kv_heads, query_rows, groups, HEAD_DIM).transpose(1, 0, 2, 3)
    return result.reshape(query_rows, kv_width * groups).astype(jnp.bfloat16)


def solution(mesh):
    in_specs = (
        P(("dp", "ctx"), "tp"),
        P(("dp", "ctx"), "tp"),
        P(("dp", "ctx"), "tp"),
        P(("dp", "ctx"), "tp"),
        P(("dp", "ctx"), "tp"),
        P("dp"),
    )
    out_specs = P(("dp", "ctx"), "tp")
    return jax.shard_map(local, mesh=mesh, in_specs=in_specs, out_specs=out_specs, check_vma=False)
```

profile of v0, /device:TPU:26, one launch (start us, length us, event | category | flops | bytes accessed | tf_op | source)
XLA Modules:
  0.0 315.2 jit_solution(11494170343296880168)
XLA Ops:
  5.9 308.3 %while.22 = (s32[]{:T(128)}, f32[2,512]{1,0:T(2,128)S(1)}, f32[2,512]{1,0:T(2,128)S(1)}, f32[2,512,128]{2,1,0:T(8,128)S(1)}, bf16[2,2,576,128]{3,2,1,0:T(8,128)(...) while((s32[]{:T(128)}, f32[2,512]{1,0:T(2,128)S(1)}, ...), condition=%wide.region_5.6_spmd.clone, body=%wide.region_2.5_spmd.clone.sunk | while | flops 310519104 | bytes 13773910 | solution.py:90
  5.9 1.9 collective-permute-start
  8.8 17.2 %collective-permute-done = bf16[2,2,576,128]{3,2,1,0:T(8,128)(2,1)S(1)} collective-permute-done((bf16[2,2,576,128]{3,2,1,0:T(8,128)(2,1)S(1)}, bf16[2,2,576,128]{3,2,1,0:T(8,128)(2,1)S(1)}, u32[]{:S(2)}, u32[]{:S(2)}) %collective-permute-start) | collective-permute-done | bytes 589856 | tf_op jit(solution)/shard_map/while/body/eval_jaxpr/ppermute | solution.py:12
  28.7 1.9 collective-permute-start
  31.6 14.9 %collective-permute-done = bf16[2,2,576,128]{3,2,1,0:T(8,128)(2,1)S(1)} collective-permute-done((bf16[2,2,576,128]{3,2,1,0:T(8,128)(2,1)S(1)}, bf16[2,2,576,128]{3,2,1,0:T(8,128)(2,1)S(1)}, u32[]{:S(2)}, u32[]{:S(2)}) %collective-permute-start) | collective-permute-done | bytes 589856 | tf_op jit(solution)/shard_map/while/body/eval_jaxpr/ppermute | solution.py:12
  49.1 1.9 collective-permute-start
  52.0 14.9 %collective-permute-done = bf16[2,2,576,128]{3,2,1,0:T(8,128)(2,1)S(1)} collective-permute-done((bf16[2,2,576,128]{3,2,1,0:T(8,128)(2,1)S(1)}, bf16[2,2,576,128]{3,2,1,0:T(8,128)(2,1)S(1)}, u32[]{:S(2)}, u32[]{:S(2)}) %collective-permute-start) | collective-permute-done | bytes 589856 | tf_op jit(solution)/shard_map/while/body/eval_jaxpr/ppermute | solution.py:12
  72.4 14.9 %collective-permute-done = bf16[2,2,576,128]{3,2,1,0:T(8,128)(2,1)S(1)} collective-permute-done((bf16[2,2,576,128]{3,2,1,0:T(8,128)(2,1)S(1)}, bf16[2,2,576,128]{3,2,1,0:T(8,128)(2,1)S(1)}, u32[]{:S(2)}, u32[]{:S(2)}) %collective-permute-start) | collective-permute-done | bytes 589856 | tf_op jit(solution)/shard_map/while/body/eval_jaxpr/ppermute | solution.py:12
  89.8 1.9 collective-permute-start
  92.8 14.9 %collective-permute-done = bf16[2,2,576,128]{3,2,1,0:T(8,128)(2,1)S(1)} collective-permute-done((bf16[2,2,576,128]{3,2,1,0:T(8,128)(2,1)S(1)}, bf16[2,2,576,128]{3,2,1,0:T(8,128)(2,1)S(1)}, u32[]{:S(2)}, u32[]{:S(2)}) %collective-permute-start) | collective-permute-done | bytes 589856 | tf_op jit(solution)/shard_map/while/body/eval_jaxpr/ppermute | solution.py:12
  113.2 14.9 %collective-permute-done = bf16[2,2,576,128]{3,2,1,0:T(8,128)(2,1)S(1)} collective-permute-done((bf16[2,2,576,128]{3,2,1,0:T(8,128)(2,1)S(1)}, bf16[2,2,576,128]{3,2,1,0:T(8,128)(2,1)S(1)}, u32[]{:S(2)}, u32[]{:S(2)}) %collective-permute-start) | collective-permute-done | bytes 589856 | tf_op jit(solution)/shard_map/while/body/eval_jaxpr/ppermute | solution.py:12
  130.6 1.9 collective-permute-start
  133.6 14.9 %collective-permute-done = bf16[2,2,576,128]{3,2,1,0:T(8,128)(2,1)S(1)} collective-permute-done((bf16[2,2,576,128]{3,2,1,0:T(8,128)(2,1)S(1)}, bf16[2,2,576,128]{3,2,1,0:T(8,128)(2,1)S(1)}, u32[]{:S(2)}, u32[]{:S(2)}) %collective-permute-start) | collective-permute-done | bytes 589856 | tf_op jit(solution)/shard_map/while/body/eval_jaxpr/ppermute | solution.py:12
  154.0 14.9 %collective-permute-done = bf16[2,2,576,128]{3,2,1,0:T(8,128)(2,1)S(1)} collective-permute-done((bf16[2,2,576,128]{3,2,1,0:T(8,128)(2,1)S(1)}, bf16[2,2,576,128]{3,2,1,0:T(8,128)(2,1)S(1)}, u32[]{:S(2)}, u32[]{:S(2)}) %collective-permute-start) | collective-permute-done | bytes 589856 | tf_op jit(solution)/shard_map/while/body/eval_jaxpr/ppermute | solution.py:12
  171.4 1.9 collective-permute-start
  174.4 14.9 %collective-permute-done = bf16[2,2,576,128]{3,2,1,0:T(8,128)(2,1)S(1)} collective-permute-done((bf16[2,2,576,128]{3,2,1,0:T(8,128)(2,1)S(1)}, bf16[2,2,576,128]{3,2,1,0:T(8,128)(2,1)S(1)}, u32[]{:S(2)}, u32[]{:S(2)}) %collective-permute-start) | collective-permute-done | bytes 589856 | tf_op jit(solution)/shard_map/while/body/eval_jaxpr/ppermute | solution.py:12
  194.8 14.9 %collective-permute-done = bf16[2,2,576,128]{3,2,1,0:T(8,128)(2,1)S(1)} collective-permute-done((bf16[2,2,576,128]{3,2,1,0:T(8,128)(2,1)S(1)}, bf16[2,2,576,128]{3,2,1,0:T(8,128)(2,1)S(1)}, u32[]{:S(2)}, u32[]{:S(2)}) %collective-permute-start) | collective-permute-done | bytes 589856 | tf_op jit(solution)/shard_map/while/body/eval_jaxpr/ppermute | solution.py:12
  212.2 1.9 collective-permute-start
  215.2 14.9 %collective-permute-done = bf16[2,2,576,128]{3,2,1,0:T(8,128)(2,1)S(1)} collective-permute-done((bf16[2,2,576,128]{3,2,1,0:T(8,128)(2,1)S(1)}, bf16[2,2,576,128]{3,2,1,0:T(8,128)(2,1)S(1)}, u32[]{:S(2)}, u32[]{:S(2)}) %collective-permute-start) | collective-permute-done | bytes 589856 | tf_op jit(solution)/shard_map/while/body/eval_jaxpr/ppermute | solution.py:12
  235.6 14.9 %collective-permute-done = bf16[2,2,576,128]{3,2,1,0:T(8,128)(2,1)S(1)} collective-permute-done((bf16[2,2,576,128]{3,2,1,0:T(8,128)(2,1)S(1)}, bf16[2,2,576,128]{3,2,1,0:T(8,128)(2,1)S(1)}, u32[]{:S(2)}, u32[]{:S(2)}) %collective-permute-start) | collective-permute-done | bytes 589856 | tf_op jit(solution)/shard_map/while/body/eval_jaxpr/ppermute | solution.py:12
  253.0 1.9 collective-permute-start
  256.0 14.9 %collective-permute-done = bf16[2,2,576,128]{3,2,1,0:T(8,128)(2,1)S(1)} collective-permute-done((bf16[2,2,576,128]{3,2,1,0:T(8,128)(2,1)S(1)}, bf16[2,2,576,128]{3,2,1,0:T(8,128)(2,1)S(1)}, u32[]{:S(2)}, u32[]{:S(2)}) %collective-permute-start) | collective-permute-done | bytes 589856 | tf_op jit(solution)/shard_map/while/body/eval_jaxpr/ppermute | solution.py:12
  276.4 14.9 %collective-permute-done = bf16[2,2,576,128]{3,2,1,0:T(8,128)(2,1)S(1)} collective-permute-done((bf16[2,2,576,128]{3,2,1,0:T(8,128)(2,1)S(1)}, bf16[2,2,576,128]{3,2,1,0:T(8,128)(2,1)S(1)}, u32[]{:S(2)}, u32[]{:S(2)}) %collective-permute-start) | collective-permute-done | bytes 589856 | tf_op jit(solution)/shard_map/while/body/eval_jaxpr/ppermute | solution.py:12
  296.7 14.9 %collective-permute-done = bf16[2,2,576,128]{3,2,1,0:T(8,128)(2,1)S(1)} collective-permute-done((bf16[2,2,576,128]{3,2,1,0:T(8,128)(2,1)S(1)}, bf16[2,2,576,128]{3,2,1,0:T(8,128)(2,1)S(1)}, u32[]{:S(2)}, u32[]{:S(2)}) %collective-permute-start) | collective-permute-done | bytes 589856 | tf_op jit(solution)/shard_map/while/body/eval_jaxpr/ppermute | solution.py:12
  (195 shorter events, 72.3 us)
Async XLA Ops:
  1.0 2.4 copy-start
  5.9 20.2 %collective-permute-start = (bf16[2,2,576,128]{3,2,1,0:T(8,128)(2,1)S(1)}, bf16[2,2,576,128]{3,2,1,0:T(8,128)(2,1)S(1)}, u32[]{:S(2)}, u32[]{:S(2)}) collective-permute-start(bf16[2,2,576,128]{3,2,1,0:T(8,128)(2,1)S(1)} %get-tuple-element.367), channel_id=1, source_target_pairs={{0,32},{32,64},{64,96},{96,128},{128,160},{160,192},{192,224},{224... | collective-permute-start | bytes 1769480 | tf_op jit(solution)/shard_map/while/body/eval_jaxpr/ppermute | solution.py:12
  28.7 17.8 %collective-permute-start = (bf16[2,2,576,128]{3,2,1,0:T(8,128)(2,1)S(1)}, bf16[2,2,576,128]{3,2,1,0:T(8,128)(2,1)S(1)}, u32[]{:S(2)}, u32[]{:S(2)}) collective-permute-start(bf16[2,2,576,128]{3,2,1,0:T(8,128)(2,1)S(1)} %get-tuple-element.367), channel_id=1, source_target_pairs={{0,32},{32,64},{64,96},{96,128},{128,160},{160,192},{192,224},{224... | collective-permute-start | bytes 1769480 | tf_op jit(solution)/shard_map/while/body/eval_jaxpr/ppermute | solution.py:12
  49.1 17.8 %collective-permute-start = (bf16[2,2,576,128]{3,2,1,0:T(8,128)(2,1)S(1)}, bf16[2,2,576,128]{3,2,1,0:T(8,128)(2,1)S(1)}, u32[]{:S(2)}, u32[]{:S(2)}) collective-permute-start(bf16[2,2,576,128]{3,2,1,0:T(8,128)(2,1)S(1)} %get-tuple-element.367), channel_id=1, source_target_pairs={{0,32},{32,64},{64,96},{96,128},{128,160},{160,192},{192,224},{224... | collective-permute-start | bytes 1769480 | tf_op jit(solution)/shard_map/while/body/eval_jaxpr/ppermute | solution.py:12
  69.4 17.8 %collective-permute-start = (bf16[2,2,576,128]{3,2,1,0:T(8,128)(2,1)S(1)}, bf16[2,2,576,128]{3,2,1,0:T(8,128)(2,1)S(1)}, u32[]{:S(2)}, u32[]{:S(2)}) collective-permute-start(bf16[2,2,576,128]{3,2,1,0:T(8,128)(2,1)S(1)} %get-tuple-element.367), channel_id=1, source_target_pairs={{0,32},{32,64},{64,96},{96,128},{128,160},{160,192},{192,224},{224... | collective-permute-start | bytes 1769480 | tf_op jit(solution)/shard_map/while/body/eval_jaxpr/ppermute | solution.py:12
  89.8 17.8 %collective-permute-start = (bf16[2,2,576,128]{3,2,1,0:T(8,128)(2,1)S(1)}, bf16[2,2,576,128]{3,2,1,0:T(8,128)(2,1)S(1)}, u32[]{:S(2)}, u32[]{:S(2)}) collective-permute-start(bf16[2,2,576,128]{3,2,1,0:T(8,128)(2,1)S(1)} %get-tuple-element.367), channel_id=1, source_target_pairs={{0,32},{32,64},{64,96},{96,128},{128,160},{160,192},{192,224},{224... | collective-permute-start | bytes 1769480 | tf_op jit(solution)/shard_map/while/body/eval_jaxpr/ppermute | solution.py:12
  110.2 17.8 %collective-permute-start = (bf16[2,2,576,128]{3,2,1,0:T(8,128)(2,1)S(1)}, bf16[2,2,576,128]{3,2,1,0:T(8,128)(2,1)S(1)}, u32[]{:S(2)}, u32[]{:S(2)}) collective-permute-start(bf16[2,2,576,128]{3,2,1,0:T(8,128)(2,1)S(1)} %get-tuple-element.367), channel_id=1, source_target_pairs={{0,32},{32,64},{64,96},{96,128},{128,160},{160,192},{192,224},{224... | collective-permute-start | bytes 1769480 | tf_op jit(solution)/shard_map/while/body/eval_jaxpr/ppermute | solution.py:12
  130.6 17.8 %collective-permute-start = (bf16[2,2,576,128]{3,2,1,0:T(8,128)(2,1)S(1)}, bf16[2,2,576,128]{3,2,1,0:T(8,128)(2,1)S(1)}, u32[]{:S(2)}, u32[]{:S(2)}) collective-permute-start(bf16[2,2,576,128]{3,2,1,0:T(8,128)(2,1)S(1)} %get-tuple-element.367), channel_id=1, source_target_pairs={{0,32},{32,64},{64,96},{96,128},{128,160},{160,192},{192,224},{224... | collective-permute-start | bytes 1769480 | tf_op jit(solution)/shard_map/while/body/eval_jaxpr/ppermute | solution.py:12
  151.0 17.8 %collective-permute-start = (bf16[2,2,576,128]{3,2,1,0:T(8,128)(2,1)S(1)}, bf16[2,2,576,128]{3,2,1,0:T(8,128)(2,1)S(1)}, u32[]{:S(2)}, u32[]{:S(2)}) collective-permute-start(bf16[2,2,576,128]{3,2,1,0:T(8,128)(2,1)S(1)} %get-tuple-element.367), channel_id=1, source_target_pairs={{0,32},{32,64},{64,96},{96,128},{128,160},{160,192},{192,224},{224... | collective-permute-start | bytes 1769480 | tf_op jit(solution)/shard_map/while/body/eval_jaxpr/ppermute | solution.py:12
  171.4 17.8 %collective-permute-start = (bf16[2,2,576,128]{3,2,1,0:T(8,128)(2,1)S(1)}, bf16[2,2,576,128]{3,2,1,0:T(8,128)(2,1)S(1)}, u32[]{:S(2)}, u32[]{:S(2)}) collective-permute-start(bf16[2,2,576,128]{3,2,1,0:T(8,128)(2,1)S(1)} %get-tuple-element.367), channel_id=1, source_target_pairs={{0,32},{32,64},{64,96},{96,128},{128,160},{160,192},{192,224},{224... | collective-permute-start | bytes 1769480 | tf_op jit(solution)/shard_map/while/body/eval_jaxpr/ppermute | solution.py:12
  191.8 17.8 %collective-permute-start = (bf16[2,2,576,128]{3,2,1,0:T(8,128)(2,1)S(1)}, bf16[2,2,576,128]{3,2,1,0:T(8,128)(2,1)S(1)}, u32[]{:S(2)}, u32[]{:S(2)}) collective-permute-start(bf16[2,2,576,128]{3,2,1,0:T(8,128)(2,1)S(1)} %get-tuple-element.367), channel_id=1, source_target_pairs={{0,32},{32,64},{64,96},{96,128},{128,160},{160,192},{192,224},{224... | collective-permute-start | bytes 1769480 | tf_op jit(solution)/shard_map/while/body/eval_jaxpr/ppermute | solution.py:12
  212.2 17.8 %collective-permute-start = (bf16[2,2,576,128]{3,2,1,0:T(8,128)(2,1)S(1)}, bf16[2,2,576,128]{3,2,1,0:T(8,128)(2,1)S(1)}, u32[]{:S(2)}, u32[]{:S(2)}) collective-permute-start(bf16[2,2,576,128]{3,2,1,0:T(8,128)(2,1)S(1)} %get-tuple-element.367), channel_id=1, source_target_pairs={{0,32},{32,64},{64,96},{96,128},{128,160},{160,192},{192,224},{224... | collective-permute-start | bytes 1769480 | tf_op jit(solution)/shard_map/while/body/eval_jaxpr/ppermute | solution.py:12
  232.6 17.8 %collective-permute-start = (bf16[2,2,576,128]{3,2,1,0:T(8,128)(2,1)S(1)}, bf16[2,2,576,128]{3,2,1,0:T(8,128)(2,1)S(1)}, u32[]{:S(2)}, u32[]{:S(2)}) collective-permute-start(bf16[2,2,576,128]{3,2,1,0:T(8,128)(2,1)S(1)} %get-tuple-element.367), channel_id=1, source_target_pairs={{0,32},{32,64},{64,96},{96,128},{128,160},{160,192},{192,224},{224... | collective-permute-start | bytes 1769480 | tf_op jit(solution)/shard_map/while/body/eval_jaxpr/ppermute | solution.py:12
  253.0 17.8 %collective-permute-start = (bf16[2,2,576,128]{3,2,1,0:T(8,128)(2,1)S(1)}, bf16[2,2,576,128]{3,2,1,0:T(8,128)(2,1)S(1)}, u32[]{:S(2)}, u32[]{:S(2)}) collective-permute-start(bf16[2,2,576,128]{3,2,1,0:T(8,128)(2,1)S(1)} %get-tuple-element.367), channel_id=1, source_target_pairs={{0,32},{32,64},{64,96},{96,128},{128,160},{160,192},{192,224},{224... | collective-permute-start | bytes 1769480 | tf_op jit(solution)/shard_map/while/body/eval_jaxpr/ppermute | solution.py:12
  273.4 17.8 %collective-permute-start = (bf16[2,2,576,128]{3,2,1,0:T(8,128)(2,1)S(1)}, bf16[2,2,576,128]{3,2,1,0:T(8,128)(2,1)S(1)}, u32[]{:S(2)}, u32[]{:S(2)}) collective-permute-start(bf16[2,2,576,128]{3,2,1,0:T(8,128)(2,1)S(1)} %get-tuple-element.367), channel_id=1, source_target_pairs={{0,32},{32,64},{64,96},{96,128},{128,160},{160,192},{192,224},{224... | collective-permute-start | bytes 1769480 | tf_op jit(solution)/shard_map/while/body/eval_jaxpr/ppermute | solution.py:12
  293.8 17.8 %collective-permute-start = (bf16[2,2,576,128]{3,2,1,0:T(8,128)(2,1)S(1)}, bf16[2,2,576,128]{3,2,1,0:T(8,128)(2,1)S(1)}, u32[]{:S(2)}, u32[]{:S(2)}) collective-permute-start(bf16[2,2,576,128]{3,2,1,0:T(8,128)(2,1)S(1)} %get-tuple-element.367), channel_id=1, source_target_pairs={{0,32},{32,64},{64,96},{96,128},{128,160},{160,192},{192,224},{224... | collective-permute-start | bytes 1769480 | tf_op jit(solution)/shard_map/while/body/eval_jaxpr/ppermute | solution.py:12
where the time goes:
time: 316 us; the launch traced here: 315 us
  waiting for transfers between devices  225 us (71%)
  matrix products  29.4 us (9%)
  starting transfers between devices  28.8 us (9%)
  other arithmetic  27.7 us (9%)
    ppermute x15, waiting for transfers between devices, passed_along(): return lax.ppermute(value, axis, pairs)  225 us
    ppermute x15, starting transfers between devices, passed_along(): return lax.ppermute(value, axis, pairs)  28.8 us
    dot_general x16, matrix products, softmax_block(): jnp.einsum('hrk,hkd->hrd', weights.astype(jnp.bfloat16), kv_block[1], pre...  19.8 us
    reduce_sum x16, other arithmetic, softmax_block(): new_total = old_total * rescale + jnp.sum(weights, -1)  10.2 us
    lt x16, other arithmetic, allowed_for(): cache_pos < length  9.8 us
    dot_general x16, matrix products, softmax_block(): jnp.einsum('hrd,hkd->hrk', query_heads, kv_block[0], preferred_element_ty...  9.61 us
  transfers between devices with their start and end apart: 15, of which 15 were waited for; matrix products, arithmetic and copies ran while one was open for 5% of the time, Pallas kernels for 0%

commit v1 on v0

v1 whole, which is shorter than its diff:
```python
import functools

import jax
import jax.numpy as jnp
from jax import lax
from jax.experimental import pallas as pl
from jax.experimental.pallas import tpu as pltpu
from jax.sharding import PartitionSpec as P

HEAD_DIM = 128
LOG2_E = 1.4426950408889634
MASKED = -1e30
TILE = 256


def kernel(chips, length_ref, q_ref, ck_ref, cv_ref, nk_ref, nv_ref, out_ref,
           held, qs, tops, totals, acc, local_sem, left_sem, right_sem, mate_sem, recv_sem):
    me = lax.axis_index("ctx")
    chip = me // 2
    core = me % 2
    cache_rows = ck_ref.shape[0]
    new_rows = nk_ref.shape[0]
    key_rows = cache_rows + new_rows
    width = ck_ref.shape[1]
    tiles = qs.shape[0]
    tiles_per_kv = tiles // (width // HEAD_DIM)
    heads = q_ref.shape[1] // HEAD_DIM
    heads_per_tile = TILE // new_rows
    length = length_ref[0]
    scale = (HEAD_DIM ** -0.5) * LOG2_E

    loads = []
    for n, (src, first, rows) in enumerate((
        (ck_ref, 0, cache_rows), (nk_ref, cache_rows, new_rows),
        (cv_ref, key_rows, cache_rows), (nv_ref, key_rows + cache_rows, new_rows),
    )):
        load = pltpu.make_async_copy(src, held.at[me, pl.ds(first, rows)], local_sem.at[n])
        load.start()
        loads.append(load)

    barrier = pltpu.get_barrier_semaphore()
    pl.semaphore_signal(barrier, inc=1, device_id={"ctx": chip * 2 + 1 - core})

    @pl.when(chip > 0)
    def _():
        pl.semaphore_signal(barrier, inc=1, device_id={"ctx": me - 2})

    @pl.when(chip < chips - 1)
    def _():
        pl.semaphore_signal(barrier, inc=1, device_id={"ctx": me + 2})

    pl.semaphore_wait(
        barrier, 1 + (chip > 0).astype(jnp.int32) + (chip < chips - 1).astype(jnp.int32))

    def copy_of(block, half, sems, target):
        part = held.at[block, pl.ds(half * key_rows, key_rows)]
        return pltpu.make_async_remote_copy(
            src_ref=part, dst_ref=part, send_sem=sems.at[block // 2, half],
            recv_sem=recv_sem.at[block, half], device_id={"ctx": target})

    def to_left(block, half):
        return copy_of(block, half, left_sem, me - 2)

    def to_right(block, half):
        return copy_of(block, half, right_sem, me + 2)

    def to_mate(block, half):
        return copy_of(block, half, mate_sem, chip * 2 + 1 - core)

    def compute(block):
        def one_tile(n, carry):
            col = pl.multiple_of((n // tiles_per_kv) * HEAD_DIM, HEAD_DIM)
            keys = held[block, 0:key_rows, pl.ds(col, HEAD_DIM)]
            values = held[block, key_rows:2 * key_rows, pl.ds(col, HEAD_DIM)]
            scores = lax.dot_general(
                keys, qs[n], (((1,), (1,)), ((), ())),
                preferred_element_type=jnp.float32) * scale
            row = lax.broadcasted_iota(jnp.int32, (cache_rows, TILE), 0)
            cached = jnp.where(row + block * cache_rows < length, scores[:cache_rows], MASKED)
            new_row = lax.broadcasted_iota(jnp.int32, (new_rows, TILE), 0)
            token = lax.broadcasted_iota(jnp.int32, (new_rows, TILE), 1) % new_rows
            fresh = jnp.where(
                new_row + block * new_rows <= token + me * new_rows, scores[cache_rows:], MASKED)
            old_top = tops[n]
            top = jnp.maximum(jnp.max(cached, 0, keepdims=True), jnp.max(fresh, 0, keepdims=True))
            top = jnp.maximum(old_top, top)
            weights = jnp.exp2(jnp.concatenate([cached, fresh], 0) - top)
            rescale = jnp.exp2(old_top - top)
            tops[n] = top
            totals[n] = totals[n] * rescale + jnp.sum(weights, 0, keepdims=True)
            acc[n] = acc[n] * rescale + lax.dot_general(
                values, weights.astype(jnp.bfloat16), (((0,), (0,)), ((), ())),
                preferred_element_type=jnp.float32)
            return carry

        lax.fori_loop(0, tiles, one_tile, 0)

    def meet(block):
        return to_mate(block, 0), to_mate(block, 1)

    for half in range(2):
        loads[2 * half].wait()
        loads[2 * half + 1].wait()

        @pl.when(chip > 0)
        def _():
            to_left(me, half).start()

        @pl.when(chip < chips - 1)
        def _():
            to_right(me, half).start()

        to_mate(me, half).start()

    for head in range(heads):
        tile, at = divmod(head, heads_per_tile)
        qs[tile, at * new_rows:(at + 1) * new_rows, :] = q_ref[:, head * HEAD_DIM:(head + 1) * HEAD_DIM]
    tops[...] = jnp.full_like(tops, MASKED)
    totals[...] = jnp.zeros_like(totals)
    acc[...] = jnp.zeros_like(acc)
    compute(me)

    def mates(at_chip):
        return at_chip * 2 + 1 - core

    def take(at_chip):
        def one(n, carry):
            block = at_chip * 2 + jnp.where(n == 0, core, 1 - core)

            @pl.when(n == 1)
            def _():
                for copy in meet(block):
                    copy.wait_recv()

            compute(block)
            return carry
        lax.fori_loop(0, 2, one, 0)

    for copy in meet(mates(chip)):
        copy.wait_recv()
    compute(mates(chip))

    def pass_on(step, half):
        @pl.when(chip + step < chips)
        def _():
            block = me + 2 * step
            to_mate(block, half).wait_recv()

            @pl.when(chip > 0)
            def _():
                to_left(block, half).start()

            to_mate(block, half).start()

        @pl.when(chip - step >= 0)
        def _():
            block = me - 2 * step
            to_mate(block, half).wait_recv()

            @pl.when(chip < chips - 1)
            def _():
                to_right(block, half).start()

            to_mate(block, half).start()

    def one_step(step, carry):
        for half in range(2):
            @pl.when(step < chips)
            def _():
                pass_on(step, half)

            at_chip = chip + (step - 1) if half == 0 else chip - (step - 1)

            @pl.when((step > 1) & (at_chip >= 0) & (at_chip < chips))
            def _():
                take(at_chip)
        return carry

    lax.fori_loop(1, chips + 1, one_step, 0)

    for n in range(tiles):
        result = jnp.transpose(acc[n] / totals[n]).astype(jnp.bfloat16)
        for at in range(heads_per_tile):
            head = n * heads_per_tile + at
            out_ref[:, head * HEAD_DIM:(head + 1) * HEAD_DIM] = result[at * new_rows:(at + 1) * new_rows]

    def finish(at_chip, carry):
        block = at_chip * 2 + core
        for half in range(2):
            @pl.when((chip > 0) & (at_chip >= chip))
            def _():
                to_left(block, half).wait_send()

            @pl.when((chip < chips - 1) & (at_chip <= chip))
            def _():
                to_right(block, half).wait_send()

            to_mate(block, half).wait_send()
        return carry

    lax.fori_loop(0, chips, finish, 0)


def local(queries, cache_keys, cache_values, new_keys, new_values, prefix_len):
    count = lax.axis_size("ctx")
    chips = count // 2
    rows, width = queries.shape
    kv_width = cache_keys.shape[1]
    key_rows = cache_keys.shape[0] + new_keys.shape[0]
    tiles = rows * width // (HEAD_DIM * TILE)
    dma = pltpu.SemaphoreType.DMA
    anywhere = pl.BlockSpec(memory_space=pl.ANY)
    return pl.pallas_call(
        functools.partial(kernel, chips),
        out_shape=jax.ShapeDtypeStruct((rows, width), jnp.bfloat16),
        in_specs=[pl.BlockSpec(memory_space=pltpu.SMEM), pl.BlockSpec(memory_space=pltpu.VMEM)] + [anywhere] * 4,
        out_specs=pl.BlockSpec(memory_space=pltpu.VMEM),
        scratch_shapes=[
            pltpu.VMEM((count, 2 * key_rows, kv_width), jnp.bfloat16),
            pltpu.VMEM((tiles, TILE, HEAD_DIM), jnp.bfloat16),
            pltpu.VMEM((tiles, 1, TILE), jnp.float32),
            pltpu.VMEM((tiles, 1, TILE), jnp.float32),
            pltpu.VMEM((tiles, HEAD_DIM, TILE), jnp.float32),
            dma((4,)), dma((chips, 2)), dma((chips, 2)), dma((chips, 2)), dma((count, 2)),
        ],
        compiler_params=pltpu.CompilerParams(collective_id=0, has_side_effects=True),
    )(prefix_len, queries, cache_keys, cache_values, new_keys, new_values)


def solution(mesh):
    spec = P(("dp", "ctx"), "tp")
    return jax.shard_map(
        local, mesh=mesh, in_specs=(spec,) * 5 + (P("dp"),), out_specs=spec, check_vma=False)
```

time: 316 us -> 107 us (0.34)
  the two profiles are of different devices: /device:TPU:26 before, /device:TPU:1 now
where the time goes in v1:
time: 107 us; the launch traced here: 105 us
  Pallas kernels  103 us (96%)
  local copies, waits for them, and re-layouts  1.67 us (2%)
    pallas_call x1, Pallas kernels, local(): pl.pallas_call(functools.partial(kernel, chips), out_shape=jax.ShapeDtype...  103 us

profile of v1, /device:TPU:1, one launch (start us, length us, event | category | flops | bytes accessed | tf_op | source)
XLA Modules:
  0.0 105.1 jit_solution(9931549974135727786)
XLA Ops:
  0.7 102.8 %shard_map.64 = bf16[64,2048]{1,0:T(8,128)(2,1)} custom-call(s32[1]{0:T(128)S(6)} %copy.8.length_ref, bf16[64,2048]{1,0:T(8,128)(2,1)} %q_ref.1, bf16[512,256]{1,0:T(8,128)(2,1)} %ck_ref.1, bf16[512,256]{1,0:T(8,128)(2,1)} %cv_ref.1, bf16[64,256]{1,0:T(8,128)(2,1)} %nk_ref.1, bf16[64,256]{1,0:T(8,128)(2,1)} %nv_ref.1), custom_call_target="tpu_custom_call" | custom-call | tf_op jit(solution)/shard_map/pallas_call | solution.py:213
  103.4 1.7 %copy.9 = bf16[64,2048]{1,0:T(8,128)(2,1)} copy(bf16[64,2048]{1,0:T(8,128)(2,1)} %shard_map.64) | data formatting | bytes 524288

commit v2 on v1

v2 whole, which is shorter than its diff:
```python
import functools

import jax
import jax.numpy as jnp
from jax import lax
from jax.experimental import pallas as pl
from jax.experimental.pallas import tpu as pltpu
from jax.sharding import PartitionSpec as P

HEAD_DIM = 128
LOG2_E = 1.4426950408889634
MASKED = -1e30
TILE = 256


HELPED = 2


def kernel(chips, length_ref, q_ref, ck_ref, cv_ref, nk_ref, nv_ref, out_ref,
           held, qs, tops, totals, acc, q_in, o_in, o_out,
           local_sem, left_sem, right_sem, mate_sem, recv_sem, q_sems, o_sems, q_recv, o_recv):
    me = lax.axis_index("ctx")
    chip = me // 2
    core = me % 2
    last = chips - 1
    low, high = HELPED, last - HELPED
    inner = (chip >= low) & (chip <= high)
    helper = (chip == low) | (chip == high)
    helped_left, helped_right = chip < low, chip > high
    helped = helped_left | helped_right
    behind, ahead = chip, last - chip
    cache_rows = ck_ref.shape[0]
    new_rows = nk_ref.shape[0]
    key_rows = cache_rows + new_rows
    heads = q_ref.shape[1] // HEAD_DIM
    heads_per_tile = TILE // new_rows
    half_width = q_ref.shape[1] // 2
    length = length_ref[0]
    scale = (HEAD_DIM ** -0.5) * LOG2_E
    mate = chip * 2 + 1 - core
    my_helper = jnp.where(helped_left, low, high) * 2 + core
    my_slot = jnp.where(helped_left, chip, last - chip)

    def helped_device(slot):
        return jnp.where(chip == low, slot, last - slot) * 2 + core

    loads = []
    for part in range(4):
        cached, fresh = ((ck_ref, nk_ref), (cv_ref, nv_ref))[part % 2]
        cols = pl.ds((1 - part // 2) * HEAD_DIM, HEAD_DIM)
        pair = (
            pltpu.make_async_copy(
                cached.at[:, cols], held.at[me, part, pl.ds(0, cache_rows)], local_sem.at[2 * part]),
            pltpu.make_async_copy(
                fresh.at[:, cols], held.at[me, part, pl.ds(cache_rows, new_rows)], local_sem.at[2 * part + 1]),
        )
        for load in pair:
            load.start()
        loads.append(pair)

    barrier = pltpu.get_barrier_semaphore()

    def greet(device):
        pl.semaphore_signal(barrier, inc=1, device_id={"ctx": device})

    greet(mate)

    @pl.when(chip > 0)
    def _():
        greet(me - 2)

    @pl.when(chip < last)
    def _():
        greet(me + 2)

    far = helped & (my_slot < HELPED - 1)

    @pl.when(far)
    def _():
        greet(my_helper)

    @pl.when(helper)
    def _():
        for slot in range(HELPED - 1):
            greet(helped_device(slot))

    def as_int(flag):
        return flag.astype(jnp.int32)

    pl.semaphore_wait(
        barrier,
        1 + as_int(chip > 0) + as_int(chip < last) + as_int(far) + as_int(helper) * (HELPED - 1))

    def q_copy(slot, device):
        return pltpu.make_async_remote_copy(
            src_ref=q_ref.at[:, pl.ds(half_width, half_width)], dst_ref=q_in.at[slot],
            send_sem=q_sems.at[0], recv_sem=q_recv.at[slot], device_id={"ctx": device})

    def o_copy(slot, device):
        return pltpu.make_async_remote_copy(
            src_ref=o_out.at[slot], dst_ref=o_in, send_sem=o_sems.at[slot],
            recv_sem=o_recv.at[0], device_id={"ctx": device})

    @pl.when(helped)
    def _():
        q_copy(my_slot, my_helper).start()

    def copy_of(block, part, sems, target):
        piece = held.at[block, part]
        return pltpu.make_async_remote_copy(
            src_ref=piece, dst_ref=piece, send_sem=sems.at[block // 2, part],
            recv_sem=recv_sem.at[block, part], device_id={"ctx": target})

    def to_left(block, part):
        return copy_of(block, part, left_sem, me - 2)

    def to_right(block, part):
        return copy_of(block, part, right_sem, me + 2)

    def to_mate(block, part):
        return copy_of(block, part, mate_sem, mate)

    def goes_left(phase):
        return jnp.where(phase == 0, chip > low, chip > 0)

    def goes_right(phase):
        return jnp.where(phase == 0, chip < high, chip < last)

    def goes_mate(phase):
        return inner | (phase == 1)

    def compute(block, phase):
        def one_tile(n, carry):
            keys = held[block, 2 * phase]
            values = held[block, 2 * phase + 1]
            asker = jnp.where(n < 4, me, helped_device((n - 4) // 2))
            scores = lax.dot_general(
                keys, qs[n], (((1,), (1,)), ((), ())),
                preferred_element_type=jnp.float32) * scale
            row = lax.broadcasted_iota(jnp.int32, (cache_rows, TILE), 0)
            cached = jnp.where(row + block * cache_rows < length, scores[:cache_rows], MASKED)
            new_row = lax.broadcasted_iota(jnp.int32, (new_rows, TILE), 0)
            token = lax.broadcasted_iota(jnp.int32, (new_rows, TILE), 1) % new_rows
            fresh = jnp.where(
                new_row + block * new_rows <= token + asker * new_rows, scores[cache_rows:], MASKED)
            old_top = tops[n]
            top = jnp.maximum(jnp.max(cached, 0, keepdims=True), jnp.max(fresh, 0, keepdims=True))
            top = jnp.maximum(old_top, top)
            weights = jnp.exp2(jnp.concatenate([cached, fresh], 0) - top)
            rescale = jnp.exp2(old_top - top)
            tops[n] = top
            totals[n] = totals[n] * rescale + jnp.sum(weights, 0, keepdims=True)
            acc[n] = acc[n] * rescale + lax.dot_general(
                values, weights.astype(jnp.bfloat16), (((0,), (0,)), ((), ())),
                preferred_element_type=jnp.float32)
            return carry

        first = jnp.where(phase == 0, 2, 0)
        end = jnp.where(phase == 0, jnp.where(helper, 4 + 2 * HELPED, jnp.where(inner, 4, 2)), 2)
        lax.fori_loop(first, end, one_tile, 0)

    def own_sends(phase, direction):
        for part in (2 * phase, 2 * phase + 1):
            if direction == "left":
                to_left(me, part).start()
            else:
                to_right(me, part).start()

    for part in range(4):
        for load in loads[part]:
            load.wait()
        phase = part // 2
        if phase == 0:
            @pl.when(chip > low)
            def _():
                to_left(me, part).start()

            @pl.when(chip < high)
            def _():
                to_right(me, part).start()

            @pl.when(inner)
            def _():
                to_mate(me, part).start()
        else:
            @pl.when(((chip <= low) & (chip > 0)) | (chip == last))
            def _():
                to_left(me, part).start()

            @pl.when(((chip >= high) & (chip < last)) | (chip == 0))
            def _():
                to_right(me, part).start()

            to_mate(me, part).start()

    for head in range(heads):
        tile, at = divmod(head, heads_per_tile)
        qs[tile, at * new_rows:(at + 1) * new_rows, :] = q_ref[:, head * HEAD_DIM:(head + 1) * HEAD_DIM]
    tops[...] = jnp.full_like(tops, MASKED)
    totals[...] = jnp.zeros_like(totals)
    acc[...] = jnp.zeros_like(acc)

    @pl.when(helper)
    def _():
        for slot in range(HELPED):
            q_copy(slot, me).wait_recv()
            for head in range(heads // 2):
                tile, at = divmod(head, heads_per_tile)
                qs[4 + 2 * slot + tile, at * new_rows:(at + 1) * new_rows, :] = (
                    q_in[slot, :, head * HEAD_DIM:(head + 1) * HEAD_DIM])

    def take(at_chip, first_phase, phases):
        def one(n, carry):
            block = at_chip * 2 + jnp.where(n % 2 == 0, core, 1 - core)
            phase = first_phase + n // 2

            @pl.when(goes_mate(phase))
            def _():
                @pl.when(n % 2 == 1)
                def _():
                    for part in range(2):
                        to_mate(block, 2 * phase + part).wait_recv()

                compute(block, phase)
            return carry
        lax.fori_loop(0, 2 * phases, one, 0)

    take(chip, 0, 2)

    def from_left(turn):
        late = turn - 2 * ahead
        phase = jnp.where(helped_right, 1, jnp.where(turn <= behind, 0, 1))
        step = jnp.where(helped_right, late, jnp.where(turn <= behind, turn, turn - behind))
        return (step >= 1) & (step <= behind), chip - step, phase

    def from_right(turn):
        late = turn - 2 * behind
        phase = jnp.where(helped_left, 1, jnp.where(turn <= ahead, 0, 1))
        step = jnp.where(helped_left, late, jnp.where(turn <= ahead, turn, turn - ahead))
        return (step >= 1) & (step <= ahead), chip + step, phase

    def pass_on(turn, half):
        there, at_chip, phase = from_left(turn)

        @pl.when(there)
        def _():
            block, part = at_chip * 2 + core, 2 * phase + half
            to_mate(block, part).wait_recv()

            @pl.when(goes_right(phase))
            def _():
                to_right(block, part).start()

            @pl.when(goes_mate(phase))
            def _():
                to_mate(block, part).start()

        there, at_chip, phase = from_right(turn)

        @pl.when(there)
        def _():
            block, part = at_chip * 2 + core, 2 * phase + half
            to_mate(block, part).wait_recv()

            @pl.when(goes_left(phase))
            def _():
                to_left(block, part).start()

            @pl.when(goes_mate(phase))
            def _():
                to_mate(block, part).start()

    turns = max(2 * high, chips + HELPED)
    answered = chips - HELPED

    def one_turn(turn, carry):
        pass_on(turn, 0)

        @pl.when(helper & (turn == answered + 1))
        def _():
            for slot in range(HELPED):
                o_copy(slot, helped_device(slot)).start()

        there, at_chip, phase = from_left(turn - 1)

        @pl.when(there & (turn > 1))
        def _():
            take(at_chip, phase, 1)

        pass_on(turn, 1)

        @pl.when((turn == behind) & (chip < high))
        def _():
            own_sends(1, "right")

        @pl.when((turn == ahead) & (chip > low))
        def _():
            own_sends(1, "left")

        there, at_chip, phase = from_right(turn - 1)

        @pl.when(there & (turn > 1))
        def _():
            take(at_chip, phase, 1)

        @pl.when(helper & (turn == answered))
        def _():
            for slot in range(HELPED):
                for n in range(2):
                    put(o_out.at[slot], n, 4 + 2 * slot + n)
        return carry

    def put(target, place, tile):
        result = jnp.transpose(acc[tile] / totals[tile]).astype(jnp.bfloat16)
        for at in range(heads_per_tile):
            head = place * heads_per_tile + at
            target[:, head * HEAD_DIM:(head + 1) * HEAD_DIM] = result[at * new_rows:(at + 1) * new_rows]

    lax.fori_loop(1, turns + 2, one_turn, 0)

    for n in range(2):
        put(out_ref, n, n)

    @pl.when(inner)
    def _():
        for n in range(2, 4):
            put(out_ref, n, n)

    @pl.when(helped)
    def _():
        o_copy(0, my_helper).wait_recv()
        out_ref[:, half_width:] = o_in[...]
        q_copy(my_slot, my_helper).wait_send()

    @pl.when(helper)
    def _():
        for slot in range(HELPED):
            o_copy(slot, me).wait_send()

    def finish(n, carry):
        at_chip, part = n // 4, n % 4
        phase = part // 2
        block = at_chip * 2 + core

        @pl.when(goes_left(phase) & (at_chip >= chip))
        def _():
            to_left(block, part).wait_send()

        @pl.when(goes_right(phase) & (at_chip <= chip))
        def _():
            to_right(block, part).wait_send()

        @pl.when(goes_mate(phase))
        def _():
            to_mate(block, part).wait_send()
        return carry

    lax.fori_loop(0, 4 * chips, finish, 0)


def local(queries, cache_keys, cache_values, new_keys, new_values, prefix_len):
    count = lax.axis_size("ctx")
    chips = count // 2
    rows, width = queries.shape
    key_rows = cache_keys.shape[0] + new_keys.shape[0]
    tiles = 4 + 2 * HELPED
    dma = pltpu.SemaphoreType.DMA
    anywhere = pl.BlockSpec(memory_space=pl.ANY)
    return pl.pallas_call(
        functools.partial(kernel, chips),
        out_shape=jax.ShapeDtypeStruct((rows, width), jnp.bfloat16),
        in_specs=[pl.BlockSpec(memory_space=pltpu.SMEM), pl.BlockSpec(memory_space=pltpu.VMEM)] + [anywhere] * 4,
        out_specs=pl.BlockSpec(memory_space=pltpu.VMEM),
        scratch_shapes=[
            pltpu.VMEM((count, 4, key_rows, HEAD_DIM), jnp.bfloat16),
            pltpu.VMEM((tiles, TILE, HEAD_DIM), jnp.bfloat16),
            pltpu.VMEM((tiles, 1, TILE), jnp.float32),
            pltpu.VMEM((tiles, 1, TILE), jnp.float32),
            pltpu.VMEM((tiles, HEAD_DIM, TILE), jnp.float32),
            pltpu.VMEM((HELPED, rows, width // 2), jnp.bfloat16),
            pltpu.VMEM((rows, width // 2), jnp.bfloat16),
            pltpu.VMEM((HELPED, rows, width // 2), jnp.bfloat16),
            dma((8,)), dma((chips, 4)), dma((chips, 4)), dma((chips, 4)), dma((count, 4)),
            dma((1,)), dma((HELPED,)), dma((HELPED,)), dma((1,)),
        ],
        compiler_params=pltpu.CompilerParams(collective_id=0, has_side_effects=True),
    )(prefix_len, queries, cache_keys, cache_values, new_keys, new_values)


def solution(mesh):
    spec = P(("dp", "ctx"), "tp")
    return jax.shard_map(
        local, mesh=mesh, in_specs=(spec,) * 5 + (P("dp"),), out_specs=spec, check_vma=False)
```

time: 107 us -> 127 us (1.19); the launches traced: 105 us -> 126 us
  Pallas kernels: 103 us -> 124 us
    pallas_call x1, Pallas kernels: 103 us -> 124 us  [local(): pl.pallas_call(functools.partial(kernel, chips), out_shape=jax.ShapeDtype...]
where the time goes in v2:
time: 127 us; the launch traced here: 126 us
  Pallas kernels  124 us (98%)
  local copies, waits for them, and re-layouts  1.67 us (1%)
    pallas_call x1, Pallas kernels, local(): pl.pallas_call(functools.partial(kernel, chips), out_shape=jax.ShapeDtype...  124 us

profile of v2, /device:TPU:1, one launch (start us, length us, event | category | flops | bytes accessed | tf_op | source)
XLA Modules:
  0.0 126.4 jit_solution(13272887624944344368)
XLA Ops:
  0.7 124.1 %shard_map.64 = bf16[64,2048]{1,0:T(8,128)(2,1)} custom-call(s32[1]{0:T(128)S(6)} %copy.8.length_ref, bf16[64,2048]{1,0:T(8,128)(2,1)} %q_ref.1, bf16[512,256]{1,0:T(8,128)(2,1)} %ck_ref.1, bf16[512,256]{1,0:T(8,128)(2,1)} %cv_ref.1, bf16[64,256]{1,0:T(8,128)(2,1)} %nk_ref.1, bf16[64,256]{1,0:T(8,128)(2,1)} %nv_ref.1), custom_call_target="tpu_custom_call" | custom-call | tf_op jit(solution)/shard_map/pallas_call | solution.py:369
  124.7 1.7 %copy.9 = bf16[64,2048]{1,0:T(8,128)(2,1)} copy(bf16[64,2048]{1,0:T(8,128)(2,1)} %shard_map.64) | data formatting | bytes 524288

commit v3 on v2

--- a/solution.py
+++ b/solution.py
@@ -13,7 +13,7 @@
 TILE = 256
 
 
-HELPED = 2
+HELPED = 1
 
 
 def kernel(chips, length_ref, q_ref, ck_ref, cv_ref, nk_ref, nv_ref, out_ref,

time: 127 us -> 109 us (0.86)
  Pallas kernels: 124 us -> 107 us
    pallas_call x1, Pallas kernels: 124 us -> 107 us  [local(): pl.pallas_call(functools.partial(kernel, chips), out_shape=jax.ShapeDtype...]
where the time goes in v3:
time: 109 us
  Pallas kernels  107 us (98%)
  local copies, waits for them, and re-layouts  1.67 us (2%)
    pallas_call x1, Pallas kernels, local(): pl.pallas_call(functools.partial(kernel, chips), out_shape=jax.ShapeDtype...  107 us

profile of v3, /device:TPU:1, one launch (start us, length us, event | category | flops | bytes accessed | tf_op | source)
XLA Modules:
  0.0 109.0 jit_solution(3679663497375433931)
XLA Ops:
  0.7 106.7 %shard_map.64 = bf16[64,2048]{1,0:T(8,128)(2,1)} custom-call(s32[1]{0:T(128)S(6)} %copy.8.length_ref, bf16[64,2048]{1,0:T(8,128)(2,1)} %q_ref.1, bf16[512,256]{1,0:T(8,128)(2,1)} %ck_ref.1, bf16[512,256]{1,0:T(8,128)(2,1)} %cv_ref.1, bf16[64,256]{1,0:T(8,128)(2,1)} %nk_ref.1, bf16[64,256]{1,0:T(8,128)(2,1)} %nv_ref.1), custom_call_target="tpu_custom_call" | custom-call | tf_op jit(solution)/shard_map/pallas_call | solution.py:369
  107.3 1.7 %copy.9 = bf16[64,2048]{1,0:T(8,128)(2,1)} copy(bf16[64,2048]{1,0:T(8,128)(2,1)} %shard_map.64) | data formatting | bytes 524288

commit v4 on v3

--- a/solution.py
+++ b/solution.py
@@ -130,34 +130,47 @@
         return inner | (phase == 1)
 
     def compute(block, phase):
-        def one_tile(n, carry):
+        def one_pair(pair, carry):
             keys = held[block, 2 * phase]
             values = held[block, 2 * phase + 1]
-            asker = jnp.where(n < 4, me, helped_device((n - 4) // 2))
-            scores = lax.dot_general(
-                keys, qs[n], (((1,), (1,)), ((), ())),
-                preferred_element_type=jnp.float32) * scale
+            asker = jnp.where(pair < 2, me, helped_device(pair - 2))
+            both = [2 * pair, 2 * pair + 1]
+            asked = [qs[n] for n in both]
+            old_tops = [tops[n] for n in both]
+            old_totals = [totals[n] for n in both]
+            old_acc = [acc[n] for n in both]
+            limit = length - block * cache_rows
+            ahead_by = (block - asker) * new_rows
             row = lax.broadcasted_iota(jnp.int32, (cache_rows, TILE), 0)
-            cached = jnp.where(row + block * cache_rows < length, scores[:cache_rows], MASKED)
             new_row = lax.broadcasted_iota(jnp.int32, (new_rows, TILE), 0)
             token = lax.broadcasted_iota(jnp.int32, (new_rows, TILE), 1) % new_rows
-            fresh = jnp.where(
-                new_row + block * new_rows <= token + asker * new_rows, scores[cache_rows:], MASKED)
-            old_top = tops[n]
-            top = jnp.maximum(jnp.max(cached, 0, keepdims=True), jnp.max(fresh, 0, keepdims=True))
-            top = jnp.maximum(old_top, top)
-            weights = jnp.exp2(jnp.concatenate([cached, fresh], 0) - top)
-            rescale = jnp.exp2(old_top - top)
-            tops[n] = top
-            totals[n] = totals[n] * rescale + jnp.sum(weights, 0, keepdims=True)
-            acc[n] = acc[n] * rescale + lax.dot_general(
-                values, weights.astype(jnp.bfloat16), (((0,), (0,)), ((), ())),
-                preferred_element_type=jnp.float32)
+            stored = row < limit
+            seen = new_row - token <= -ahead_by
+            scores = [
+                lax.dot_general(keys, q, (((1,), (1,)), ((), ())), preferred_element_type=jnp.float32) * scale
+                for q in asked]
+            results = []
+            for n in range(2):
+                cached = jnp.where(stored, scores[n][:cache_rows], MASKED)
+                fresh = jnp.where(seen, scores[n][cache_rows:], MASKED)
+                top = jnp.maximum(jnp.max(cached, 0, keepdims=True), jnp.max(fresh, 0, keepdims=True))
+                top = jnp.maximum(old_tops[n], top)
+                weights = jnp.exp2(jnp.concatenate([cached, fresh], 0) - top)
+                rescale = jnp.exp2(old_tops[n] - top)
+                total = old_totals[n] * rescale + jnp.sum(weights, 0, keepdims=True)
+                part = lax.dot_general(
+                    values, weights.astype(jnp.bfloat16), (((0,), (0,)), ((), ())),
+                    preferred_element_type=jnp.float32)
+                results.append((top, total, old_acc[n] * rescale + part))
+            for n, (top, total, summed) in zip(both, results):
+                tops[n] = top
+                totals[n] = total
+                acc[n] = summed
             return carry
 
-        first = jnp.where(phase == 0, 2, 0)
-        end = jnp.where(phase == 0, jnp.where(helper, 4 + 2 * HELPED, jnp.where(inner, 4, 2)), 2)
-        lax.fori_loop(first, end, one_tile, 0)
+        first = jnp.where(phase == 0, 1, 0)
+        end = jnp.where(phase == 0, jnp.where(helper, 2 + HELPED, jnp.where(inner, 2, 1)), 1)
+        lax.fori_loop(first, end, one_pair, 0)
 
     def own_sends(phase, direction):
         for part in (2 * phase, 2 * phase + 1):

time: 109 us -> 104 us (0.954)
  Pallas kernels: 107 us -> 102 us
    pallas_call x1, Pallas kernels: 107 us -> 102 us  [local(): pl.pallas_call(functools.partial(kernel, chips), out_shape=jax.ShapeDtype...]
where the time goes in v4:
time: 104 us
  Pallas kernels  102 us (98%)
  local copies, waits for them, and re-layouts  1.67 us (2%)
    pallas_call x1, Pallas kernels, local(): pl.pallas_call(functools.partial(kernel, chips), out_shape=jax.ShapeDtype...  102 us

profile of v4, /device:TPU:1, one launch (start us, length us, event | category | flops | bytes accessed | tf_op | source)
XLA Modules:
  0.0 104.1 jit_solution(16164863577294576700)
XLA Ops:
  0.7 101.8 %shard_map.64 = bf16[64,2048]{1,0:T(8,128)(2,1)} custom-call(s32[1]{0:T(128)S(6)} %copy.8.length_ref, bf16[64,2048]{1,0:T(8,128)(2,1)} %q_ref.1, bf16[512,256]{1,0:T(8,128)(2,1)} %ck_ref.1, bf16[512,256]{1,0:T(8,128)(2,1)} %cv_ref.1, bf16[64,256]{1,0:T(8,128)(2,1)} %nk_ref.1, bf16[64,256]{1,0:T(8,128)(2,1)} %nv_ref.1), custom_call_target="tpu_custom_call" | custom-call | tf_op jit(solution)/shard_map/pallas_call | solution.py:382
  102.4 1.7 %copy.9 = bf16[64,2048]{1,0:T(8,128)(2,1)} copy(bf16[64,2048]{1,0:T(8,128)(2,1)} %shard_map.64) | data formatting | bytes 524288

commit v5 on v4

--- a/solution.py
+++ b/solution.py
@@ -13,19 +13,19 @@
 TILE = 256
 
 
-HELPED = 1
+HELPED = 2
 
 
 def kernel(chips, length_ref, q_ref, ck_ref, cv_ref, nk_ref, nv_ref, out_ref,
            held, qs, tops, totals, acc, q_in, o_in, o_out,
-           local_sem, left_sem, right_sem, mate_sem, recv_sem, q_sems, o_sems, q_recv, o_recv):
+           local_sem, left_sem, right_sem, mate_sem, recv_sem, q_sems, o_sems):
     me = lax.axis_index("ctx")
     chip = me // 2
     core = me % 2
     last = chips - 1
     low, high = HELPED, last - HELPED
     inner = (chip >= low) & (chip <= high)
-    helper = (chip == low) | (chip == high)
+    helper = inner & ((chip < low + HELPED) | (chip > high - HELPED))
     helped_left, helped_right = chip < low, chip > high
     helped = helped_left | helped_right
     behind, ahead = chip, last - chip
@@ -38,11 +38,8 @@
     length = length_ref[0]
     scale = (HEAD_DIM ** -0.5) * LOG2_E
     mate = chip * 2 + 1 - core
-    my_helper = jnp.where(helped_left, low, high) * 2 + core
-    my_slot = jnp.where(helped_left, chip, last - chip)
-
-    def helped_device(slot):
-        return jnp.where(chip == low, slot, last - slot) * 2 + core
+    lower = chip < chips // 2
+    partner = me + jnp.where(lower == helped, 2 * HELPED, -2 * HELPED)
 
     loads = []
     for part in range(4):
@@ -73,37 +70,29 @@
     def _():
         greet(me + 2)
 
-    far = helped & (my_slot < HELPED - 1)
+    far = (helped | helper) & (HELPED > 1)
 
     @pl.when(far)
     def _():
-        greet(my_helper)
-
-    @pl.when(helper)
-    def _():
-        for slot in range(HELPED - 1):
-            greet(helped_device(slot))
+        greet(partner)
 
     def as_int(flag):
         return flag.astype(jnp.int32)
 
     pl.semaphore_wait(
         barrier,
-        1 + as_int(chip > 0) + as_int(chip < last) + as_int(far) + as_int(helper) * (HELPED - 1))
-
-    def q_copy(slot, device):
-        return pltpu.make_async_remote_copy(
-            src_ref=q_ref.at[:, pl.ds(half_width, half_width)], dst_ref=q_in.at[slot],
-            send_sem=q_sems.at[0], recv_sem=q_recv.at[slot], device_id={"ctx": device})
-
-    def o_copy(slot, device):
-        return pltpu.make_async_remote_copy(
-            src_ref=o_out.at[slot], dst_ref=o_in, send_sem=o_sems.at[slot],
-            recv_sem=o_recv.at[0], device_id={"ctx": device})
+        1 + as_int(chip > 0) + as_int(chip < last) + as_int(far))
+
+    q_copy = pltpu.make_async_remote_copy(
+        src_ref=q_ref.at[:, pl.ds(half_width, half_width)], dst_ref=q_in,
+        send_sem=q_sems.at[0], recv_sem=q_sems.at[1], device_id={"ctx": partner})
+    o_copy = pltpu.make_async_remote_copy(
+        src_ref=o_out, dst_ref=o_in,
+        send_sem=o_sems.at[0], recv_sem=o_sems.at[1], device_id={"ctx": partner})
 
     @pl.when(helped)
     def _():
-        q_copy(my_slot, my_helper).start()
+        q_copy.start()
 
     def copy_of(block, part, sems, target):
         piece = held.at[block, part]
@@ -133,7 +122,7 @@
         def one_pair(pair, carry):
             keys = held[block, 2 * phase]
             values = held[block, 2 * phase + 1]
-            asker = jnp.where(pair < 2, me, helped_device(pair - 2))
+            asker = jnp.where(pair < 2, me, partner)
             both = [2 * pair, 2 * pair + 1]
             asked = [qs[n] for n in both]
             old_tops = [tops[n] for n in both]
@@ -169,7 +158,7 @@
             return carry
 
         first = jnp.where(phase == 0, 1, 0)
-        end = jnp.where(phase == 0, jnp.where(helper, 2 + HELPED, jnp.where(inner, 2, 1)), 1)
+        end = jnp.where(phase == 0, jnp.where(helper, 3, jnp.where(inner, 2, 1)), 1)
         lax.fori_loop(first, end, one_pair, 0)
 
     def own_sends(phase, direction):
@@ -215,12 +204,10 @@
 
     @pl.when(helper)
     def _():
-        for slot in range(HELPED):
-            q_copy(slot, me).wait_recv()
-            for head in range(heads // 2):
-                tile, at = divmod(head, heads_per_tile)
-                qs[4 + 2 * slot + tile, at * new_rows:(at + 1) * new_rows, :] = (
-                    q_in[slot, :, head * HEAD_DIM:(head + 1) * HEAD_DIM])
+        q_copy.wait_recv()
+        for head in range(heads // 2):
+            tile, at = divmod(head, heads_per_tile)
+            qs[4 + tile, at * new_rows:(at + 1) * new_rows, :] = q_in[:, head * HEAD_DIM:(head + 1) * HEAD_DIM]
 
     def take(at_chip, first_phase, phases):
         def one(n, carry):
@@ -291,8 +278,7 @@
 
         @pl.when(helper & (turn == answered + 1))
         def _():
-            for slot in range(HELPED):
-                o_copy(slot, helped_device(slot)).start()
+            o_copy.start()
 
         there, at_chip, phase = from_left(turn - 1)
 
@@ -318,9 +304,8 @@
 
         @pl.when(helper & (turn == answered))
         def _():
-            for slot in range(HELPED):
-                for n in range(2):
-                    put(o_out.at[slot], n, 4 + 2 * slot + n)
+            for n in range(2):
+                put(o_out, n, 4 + n)
         return carry
 
     def put(target, place, tile):
@@ -341,14 +326,13 @@
 
     @pl.when(helped)
     def _():
-        o_copy(0, my_helper).wait_recv()
+        o_copy.wait_recv()
         out_ref[:, half_width:] = o_in[...]
-        q_copy(my_slot, my_helper).wait_send()
+        q_copy.wait_send()
 
     @pl.when(helper)
     def _():
-        for slot in range(HELPED):
-            o_copy(slot, me).wait_send()
+        o_copy.wait_send()
 
     def finish(n, carry):
         at_chip, part = n // 4, n % 4
@@ -376,7 +360,7 @@
     chips = count // 2
     rows, width = queries.shape
     key_rows = cache_keys.shape[0] + new_keys.shape[0]
-    tiles = 4 + 2 * HELPED
+    tiles = 6
     dma = pltpu.SemaphoreType.DMA
     anywhere = pl.BlockSpec(memory_space=pl.ANY)
     return pl.pallas_call(
@@ -390,11 +374,11 @@
             pltpu.VMEM((tiles, 1, TILE), jnp.float32),
             pltpu.VMEM((tiles, 1, TILE), jnp.float32),
             pltpu.VMEM((tiles, HEAD_DIM, TILE), jnp.float32),
-            pltpu.VMEM((HELPED, rows, width // 2), jnp.bfloat16),
             pltpu.VMEM((rows, width // 2), jnp.bfloat16),
-            pltpu.VMEM((HELPED, rows, width // 2), jnp.bfloat16),
+            pltpu.VMEM((rows, width // 2), jnp.bfloat16),
+            pltpu.VMEM((rows, width // 2), jnp.bfloat16),
             dma((8,)), dma((chips, 4)), dma((chips, 4)), dma((chips, 4)), dma((count, 4)),
-            dma((1,)), dma((HELPED,)), dma((HELPED,)), dma((1,)),
+            dma((2,)), dma((2,)),
         ],
         compiler_params=pltpu.CompilerParams(collective_id=0, has_side_effects=True),
     )(prefix_len, queries, cache_keys, cache_values, new_keys, new_values)

time: 104 us -> 104 us (level)
  no operation moved by 1% of the time
where the time goes in v5:
time: 104 us
  Pallas kernels  102 us (98%)
  local copies, waits for them, and re-layouts  1.67 us (2%)
    pallas_call x1, Pallas kernels, local(): pl.pallas_call(functools.partial(kernel, chips), out_shape=jax.ShapeDtype...  102 us

profile of v5, /device:TPU:1, one launch (start us, length us, event | category | flops | bytes accessed | tf_op | source)
XLA Modules:
  0.0 104.2 jit_solution(9134013811417732119)
XLA Ops:
  0.7 101.9 %shard_map.64 = bf16[64,2048]{1,0:T(8,128)(2,1)} custom-call(s32[1]{0:T(128)S(6)} %copy.8.length_ref, bf16[64,2048]{1,0:T(8,128)(2,1)} %q_ref.1, bf16[512,256]{1,0:T(8,128)(2,1)} %ck_ref.1, bf16[512,256]{1,0:T(8,128)(2,1)} %cv_ref.1, bf16[64,256]{1,0:T(8,128)(2,1)} %nk_ref.1, bf16[64,256]{1,0:T(8,128)(2,1)} %nv_ref.1), custom_call_target="tpu_custom_call" | custom-call | tf_op jit(solution)/shard_map/pallas_call | solution.py:366
  102.6 1.7 %copy.9 = bf16[64,2048]{1,0:T(8,128)(2,1)} copy(bf16[64,2048]{1,0:T(8,128)(2,1)} %shard_map.64) | data formatting | bytes 524288

commit v6 on v5

--- a/solution.py
+++ b/solution.py
@@ -14,6 +14,7 @@
 
 
 HELPED = 2
+PIECES = 2
 
 
 def kernel(chips, length_ref, q_ref, ck_ref, cv_ref, nk_ref, nv_ref, out_ref,
@@ -94,20 +95,27 @@
     def _():
         q_copy.start()
 
-    def copy_of(block, part, sems, target):
-        piece = held.at[block, part]
+    piece_rows = key_rows // PIECES
+
+    def copy_of(block, part, sems, target, piece):
+        rows = pl.ds(0, key_rows) if piece is None else pl.ds(piece * piece_rows, piece_rows)
+        held_rows = held.at[block, part, rows]
         return pltpu.make_async_remote_copy(
-            src_ref=piece, dst_ref=piece, send_sem=sems.at[block // 2, part],
-            recv_sem=recv_sem.at[block, part], device_id={"ctx": target})
-
-    def to_left(block, part):
-        return copy_of(block, part, left_sem, me - 2)
-
-    def to_right(block, part):
-        return copy_of(block, part, right_sem, me + 2)
-
-    def to_mate(block, part):
-        return copy_of(block, part, mate_sem, mate)
+            src_ref=held_rows, dst_ref=held_rows, send_sem=sems.at[block // 2, part],
+            recv_sem=recv_sem.at[block, part * PIECES + (piece or 0)], device_id={"ctx": target})
+
+    def to_left(block, part, piece=None):
+        return copy_of(block, part, left_sem, me - 2, piece)
+
+    def to_right(block, part, piece=None):
+        return copy_of(block, part, right_sem, me + 2, piece)
+
+    def to_mate(block, part, piece=None):
+        return copy_of(block, part, mate_sem, mate, piece)
+
+    def start_all(copy, part):
+        for piece in range(PIECES):
+            copy(me, part, piece).start()
 
     def goes_left(phase):
         return jnp.where(phase == 0, chip > low, chip > 0)
@@ -164,9 +172,9 @@
     def own_sends(phase, direction):
         for part in (2 * phase, 2 * phase + 1):
             if direction == "left":
-                to_left(me, part).start()
+                start_all(to_left, part)
             else:
-                to_right(me, part).start()
+                start_all(to_right, part)
 
     for part in range(4):
         for load in loads[part]:
@@ -175,25 +183,25 @@
         if phase == 0:
             @pl.when(chip > low)
             def _():
-                to_left(me, part).start()
+                start_all(to_left, part)
 
             @pl.when(chip < high)
             def _():
-                to_right(me, part).start()
+                start_all(to_right, part)
 
             @pl.when(inner)
             def _():
-                to_mate(me, part).start()
+                start_all(to_mate, part)
         else:
             @pl.when(((chip <= low) & (chip > 0)) | (chip == last))
             def _():
-                to_left(me, part).start()
+                start_all(to_left, part)
 
             @pl.when(((chip >= high) & (chip < last)) | (chip == 0))
             def _():
-                to_right(me, part).start()
-
-            to_mate(me, part).start()
+                start_all(to_right, part)
+
+            start_all(to_mate, part)
 
     for head in range(heads):
         tile, at = divmod(head, heads_per_tile)
@@ -219,13 +227,14 @@
                 @pl.when(n % 2 == 1)
                 def _():
                     for part in range(2):
-                        to_mate(block, 2 * phase + part).wait_recv()
+                        for piece in range(PIECES):
+                            to_mate(block, 2 * phase + part, piece).wait_recv()
 
                 compute(block, phase)
             return carry
         lax.fori_loop(0, 2 * phases, one, 0)
 
-    take(chip, 0, 2)
+    take(chip, 0, 1)
 
     def from_left(turn):
         late = turn - 2 * ahead
@@ -240,35 +249,23 @@
         return (step >= 1) & (step <= ahead), chip + step, phase
 
     def pass_on(turn, half):
-        there, at_chip, phase = from_left(turn)
-
-        @pl.when(there)
-        def _():
-            block, part = at_chip * 2 + core, 2 * phase + half
-            to_mate(block, part).wait_recv()
-
-            @pl.when(goes_right(phase))
-            def _():
-                to_right(block, part).start()
-
-            @pl.when(goes_mate(phase))
-            def _():
-                to_mate(block, part).start()
-
-        there, at_chip, phase = from_right(turn)
-
-        @pl.when(there)
-        def _():
-            block, part = at_chip * 2 + core, 2 * phase + half
-            to_mate(block, part).wait_recv()
-
-            @pl.when(goes_left(phase))
-            def _():
-                to_left(block, part).start()
-
-            @pl.when(goes_mate(phase))
-            def _():
-                to_mate(block, part).start()
+        for piece in range(PIECES):
+            for coming, onward, goes in (
+                (from_left, to_right, goes_right), (from_right, to_left, goes_left)):
+                there, at_chip, phase = coming(turn)
+                block, part = at_chip * 2 + core, 2 * phase + half
+
+                @pl.when(there)
+                def _():
+                    to_mate(block, part, piece).wait_recv()
+
+                    @pl.when(goes(phase))
+                    def _():
+                        onward(block, part, piece).start()
+
+                    @pl.when(goes_mate(phase))
+                    def _():
+                        to_mate(block, part, piece).start()
 
     turns = max(2 * high, chips + HELPED)
     answered = chips - HELPED
@@ -282,9 +279,9 @@
 
         there, at_chip, phase = from_left(turn - 1)
 
-        @pl.when(there & (turn > 1))
-        def _():
-            take(at_chip, phase, 1)
+        @pl.when(there | (turn == 1))
+        def _():
+            take(jnp.where(turn == 1, chip, at_chip), jnp.where(turn == 1, 1, phase), 1)
 
         pass_on(turn, 1)
 
@@ -377,7 +374,7 @@
             pltpu.VMEM((rows, width // 2), jnp.bfloat16),
             pltpu.VMEM((rows, width // 2), jnp.bfloat16),
             pltpu.VMEM((rows, width // 2), jnp.bfloat16),
-            dma((8,)), dma((chips, 4)), dma((chips, 4)), dma((chips, 4)), dma((count, 4)),
+            dma((8,)), dma((chips, 4)), dma((chips, 4)), dma((chips, 4)), dma((count, 4 * PIECES)),
             dma((2,)), dma((2,)),
         ],
         compiler_params=pltpu.CompilerParams(collective_id=0, has_side_effects=True),

time: 104 us -> 103 us (level)
  Pallas kernels: 102 us -> 99.9 us
    pallas_call x1, Pallas kernels: 102 us -> 99.9 us  [local(): pl.pallas_call(functools.partial(kernel, chips), out_shape=jax.ShapeDtype...]
where the time goes in v6:
time: 103 us; the launch traced here: 102 us
  Pallas kernels  99.9 us (97%)
  local copies, waits for them, and re-layouts  1.67 us (2%)
    pallas_call x1, Pallas kernels, local(): pl.pallas_call(functools.partial(kernel, chips), out_shape=jax.ShapeDtype...  99.9 us

profile of v6, /device:TPU:1, one launch (start us, length us, event | category | flops | bytes accessed | tf_op | source)
XLA Modules:
  0.0 102.2 jit_solution(13416829371498306435)
XLA Ops:
  0.7 99.9 %shard_map.64 = bf16[64,2048]{1,0:T(8,128)(2,1)} custom-call(s32[1]{0:T(128)S(6)} %copy.8.length_ref, bf16[64,2048]{1,0:T(8,128)(2,1)} %q_ref.1, bf16[512,256]{1,0:T(8,128)(2,1)} %ck_ref.1, bf16[512,256]{1,0:T(8,128)(2,1)} %cv_ref.1, bf16[64,256]{1,0:T(8,128)(2,1)} %nk_ref.1, bf16[64,256]{1,0:T(8,128)(2,1)} %nv_ref.1), custom_call_target="tpu_custom_call" | custom-call | tf_op jit(solution)/shard_map/pallas_call | solution.py:363
  100.5 1.7 %copy.9 = bf16[64,2048]{1,0:T(8,128)(2,1)} copy(bf16[64,2048]{1,0:T(8,128)(2,1)} %shard_map.64) | data formatting | bytes 524288

commit v7 on v6

--- a/solution.py
+++ b/solution.py
@@ -13,7 +13,7 @@
 TILE = 256
 
 
-HELPED = 2
+HELPED = 1
 PIECES = 2
 
 

time: 103 us -> 102 us (level)
  no operation moved by 1% of the time
where the time goes in v7:
time: 102 us; the launch traced here: 101 us
  Pallas kernels  99 us (97%)
  local copies, waits for them, and re-layouts  1.67 us (2%)
    pallas_call x1, Pallas kernels, local(): pl.pallas_call(functools.partial(kernel, chips), out_shape=jax.ShapeDtype...  99 us

profile of v7, /device:TPU:1, one launch (start us, length us, event | category | flops | bytes accessed | tf_op | source)
XLA Modules:
  0.0 101.4 jit_solution(927393115003511393)
XLA Ops:
  0.7 99.0 %shard_map.64 = bf16[64,2048]{1,0:T(8,128)(2,1)} custom-call(s32[1]{0:T(128)S(6)} %copy.8.length_ref, bf16[64,2048]{1,0:T(8,128)(2,1)} %q_ref.1, bf16[512,256]{1,0:T(8,128)(2,1)} %ck_ref.1, bf16[512,256]{1,0:T(8,128)(2,1)} %cv_ref.1, bf16[64,256]{1,0:T(8,128)(2,1)} %nk_ref.1, bf16[64,256]{1,0:T(8,128)(2,1)} %nv_ref.1), custom_call_target="tpu_custom_call" | custom-call | tf_op jit(solution)/shard_map/pallas_call | solution.py:363
  99.7 1.7 %copy.9 = bf16[64,2048]{1,0:T(8,128)(2,1)} copy(bf16[64,2048]{1,0:T(8,128)(2,1)} %shard_map.64) | data formatting | bytes 524288

commit v8 on v7

--- a/solution.py
+++ b/solution.py
@@ -14,7 +14,7 @@
 
 
 HELPED = 1
-PIECES = 2
+PIECES = 4
 
 
 def kernel(chips, length_ref, q_ref, ck_ref, cv_ref, nk_ref, nv_ref, out_ref,
@@ -303,6 +303,11 @@
         def _():
             for n in range(2):
                 put(o_out, n, 4 + n)
+
+        @pl.when(inner & (turn == answered + 1))
+        def _():
+            for n in range(2, 4):
+                put(out_ref, n, n)
         return carry
 
     def put(target, place, tile):
@@ -315,11 +320,6 @@
 
     for n in range(2):
         put(out_ref, n, n)
-
-    @pl.when(inner)
-    def _():
-        for n in range(2, 4):
-            put(out_ref, n, n)
 
     @pl.when(helped)
     def _():

time: 102 us -> 104 us (1.020)
  Pallas kernels: 99 us -> 101 us
    pallas_call x1, Pallas kernels: 99 us -> 101 us  [local(): pl.pallas_call(functools.partial(kernel, chips), out_shape=jax.ShapeDtype...]
where the time goes in v8:
time: 104 us; the launch traced here: 103 us
  Pallas kernels  101 us (97%)
  local copies, waits for them, and re-layouts  1.67 us (2%)
    pallas_call x1, Pallas kernels, local(): pl.pallas_call(functools.partial(kernel, chips), out_shape=jax.ShapeDtype...  101 us

profile of v8, /device:TPU:1, one launch (start us, length us, event | category | flops | bytes accessed | tf_op | source)
XLA Modules:
  0.0 103.4 jit_solution(11939280043662721081)
XLA Ops:
  0.7 101.1 %shard_map.64 = bf16[64,2048]{1,0:T(8,128)(2,1)} custom-call(s32[1]{0:T(128)S(6)} %copy.8.length_ref, bf16[64,2048]{1,0:T(8,128)(2,1)} %q_ref.1, bf16[512,256]{1,0:T(8,128)(2,1)} %ck_ref.1, bf16[512,256]{1,0:T(8,128)(2,1)} %cv_ref.1, bf16[64,256]{1,0:T(8,128)(2,1)} %nk_ref.1, bf16[64,256]{1,0:T(8,128)(2,1)} %nv_ref.1), custom_call_target="tpu_custom_call" | custom-call | tf_op jit(solution)/shard_map/pallas_call | solution.py:363
  101.8 1.7 %copy.9 = bf16[64,2048]{1,0:T(8,128)(2,1)} copy(bf16[64,2048]{1,0:T(8,128)(2,1)} %shard_map.64) | data formatting | bytes 524288

commit v9 on v8

--- a/solution.py
+++ b/solution.py
@@ -14,7 +14,7 @@
 
 
 HELPED = 1
-PIECES = 4
+PIECES = 2
 
 
 def kernel(chips, length_ref, q_ref, ck_ref, cv_ref, nk_ref, nv_ref, out_ref,

time: 104 us -> 102 us (0.981)
  Pallas kernels: 101 us -> 99.1 us
    pallas_call x1, Pallas kernels: 101 us -> 99.1 us  [local(): pl.pallas_call(functools.partial(kernel, chips), out_shape=jax.ShapeDtype...]
where the time goes in v9:
time: 102 us; the launch traced here: 101 us
  Pallas kernels  99.1 us (97%)
  local copies, waits for them, and re-layouts  1.67 us (2%)
    pallas_call x1, Pallas kernels, local(): pl.pallas_call(functools.partial(kernel, chips), out_shape=jax.ShapeDtype...  99.1 us

profile of v9, /device:TPU:1, one launch (start us, length us, event | category | flops | bytes accessed | tf_op | source)
XLA Modules:
  0.0 101.4 jit_solution(11923652297265580715)
XLA Ops:
  0.7 99.1 %shard_map.64 = bf16[64,2048]{1,0:T(8,128)(2,1)} custom-call(s32[1]{0:T(128)S(6)} %copy.8.length_ref, bf16[64,2048]{1,0:T(8,128)(2,1)} %q_ref.1, bf16[512,256]{1,0:T(8,128)(2,1)} %ck_ref.1, bf16[512,256]{1,0:T(8,128)(2,1)} %cv_ref.1, bf16[64,256]{1,0:T(8,128)(2,1)} %nk_ref.1, bf16[64,256]{1,0:T(8,128)(2,1)} %nv_ref.1), custom_call_target="tpu_custom_call" | custom-call | tf_op jit(solution)/shard_map/pallas_call | solution.py:363
  99.7 1.7 %copy.9 = bf16[64,2048]{1,0:T(8,128)(2,1)} copy(bf16[64,2048]{1,0:T(8,128)(2,1)} %shard_map.64) | data formatting | bytes 524288
